TPU v7x, 256 devices: a whole 4x4x8 slice. The times are simulated.
256 devices in a mesh: enc: 16 (over z, core), seq: 16 (over y, x).
Axes of the slice: x: 4, y: 4, z: 8, core: 2. Of those that a mesh axis runs over, the one named last changes fastest.
Arguments:
- queries: bfloat16 [16, 2048, 8192], P('enc', 'seq'), may hold values from -160 to 160
- kv_pool: bfloat16 [128, 2, 128, 8192], P('enc', None, None, 'seq'), may hold values from -16 to 16
- send_lists: int32 [16, 16, 1], P('enc'), may hold values from 0 to 7, as said below
- block_slots: int32 [16, 32, 2], P('enc'), may hold values from 0 to 15, as said below
- grad_context: bfloat16 [16, 2048, 8192], P('enc', 'seq'), may hold values from -24 to 24
Outputs:
- context: bfloat16 [16, 2048, 8192], P('enc', 'seq')
- grad_queries: bfloat16 [16, 2048, 8192], P('enc', 'seq')
- grad_pool: bfloat16 [128, 2, 128, 8192], P('enc', None, None, 'seq')
Inputs may be any that keep to these rules, and one draw needn't show every extreme that they name: send_lists[o, e] names 1 different local entries; each of a shard's 8 entries is named for at least one sequence. `block_slots`: the two slots of a block differ; every slot of a sequence is named by at least one of its blocks.
All inputs are finite; a program needn't handle non-finite values.
Results may differ from a plain program's by a relative error of at most 0.0065.
Values may be sent and summed in bfloat16 or wider, within the bound.
A program may use at most 128 MiB of HBM per device.

v0:
```python
import jax
import jax.numpy as jnp
from jax import lax
from jax.sharding import PartitionSpec as P

DH = 128
BLOCK = 64
NBLEN = 128


def to_heads(token_major):
    return lax.all_to_all(token_major, "seq", split_axis=2, concat_axis=1, tiled=True)


def to_tokens(head_major):
    return lax.all_to_all(head_major, "seq", split_axis=1, concat_axis=2, tiled=True)


def fetch_slots(kv_pool, entries):
    outgoing = kv_pool[entries]
    arrived = lax.all_to_all(outgoing, "enc", split_axis=0, concat_axis=0, tiled=True)
    return arrived.reshape((-1,) + kv_pool.shape[1:])


def move_up(row_data):
    filler = jnp.zeros((BLOCK - 1, row_data.shape[1]), row_data.dtype)
    return jnp.concatenate([row_data[BLOCK - 1 :], filler], axis=0)


def move_down(row_data):
    filler = jnp.zeros((BLOCK - 1, row_data.shape[1]), row_data.dtype)
    return jnp.concatenate([filler, row_data[: row_data.shape[0] - BLOCK + 1]], axis=0)


def into_blocks(head_rows, heads_here):
    blocks = head_rows.shape[0] // BLOCK
    return move_up(head_rows).reshape(blocks, BLOCK, heads_here, DH).transpose(0, 2, 1, 3)


def out_of_blocks(block_rows):
    blocks, heads_here = (block_rows.shape[0], block_rows.shape[1])
    return move_down(block_rows.transpose(0, 2, 1, 3).reshape(blocks * BLOCK, heads_here * DH))


def forward_parts(head_rows, arrived, block_use):
    slots = arrived.shape[0]
    heads_here = arrived.shape[-1] // DH
    queries_moved = into_blocks(head_rows, heads_here)
    pool_heads = arrived.reshape(slots, 2, NBLEN, heads_here, DH).transpose(0, 1, 3, 2, 4)
    keys_used = [pool_heads[:, 0][block_use[:, 0]], pool_heads[:, 0][block_use[:, 1]]]
    values_used = [pool_heads[:, 1][block_use[:, 0]], pool_heads[:, 1][block_use[:, 1]]]
    scores = [
        jnp.einsum("chid,chjd->chij", queries_moved, keys, preferred_element_type=jnp.float32)
        * DH ** (-0.5)
        for keys in keys_used
    ]
    row_peak = jnp.maximum(
        jnp.max(scores[0], axis=-1, keepdims=True), jnp.max(scores[1], axis=-1, keepdims=True)
    )
    weights = [jnp.exp(part_scores - row_peak) for part_scores in scores]
    total = jnp.sum(weights[0], axis=-1, keepdims=True) + jnp.sum(
        weights[1], axis=-1, keepdims=True
    )
    row_probs = [part_weights / total for part_weights in weights]
    probs_low = [part_probs.astype(jnp.bfloat16) for part_probs in row_probs]
    return (queries_moved, keys_used, values_used, row_probs, probs_low)


def local(queries, kv_pool, send_lists, block_slots, grad_context):
    block_use = block_slots[0]
    entries = send_lists[0]
    head_width = kv_pool.shape[-1]
    heads_here = head_width // DH
    score_scale = DH ** (-0.5)
    arrived = fetch_slots(kv_pool, entries)
    slots = arrived.shape[0]
    queries_moved, keys_used, values_used, row_probs, probs_low = forward_parts(
        to_heads(queries)[0], arrived, block_use
    )
    out_blocks = jnp.einsum(
        "chij,chjd->chid", probs_low[0], values_used[0], preferred_element_type=jnp.float32
    )
    out_blocks = out_blocks + jnp.einsum(
        "chij,chjd->chid", probs_low[1], values_used[1], preferred_element_type=jnp.float32
    )
    context = to_tokens(out_of_blocks(out_blocks.astype(jnp.bfloat16))[None])
    head_grads = to_heads(grad_context)[0]
    grads_moved = into_blocks(head_grads, heads_here)
    grad_probs = [
        jnp.einsum("chid,chjd->chij", grads_moved, values, preferred_element_type=jnp.float32)
        for values in values_used
    ]
    row_inner = jnp.sum(row_probs[0] * grad_probs[0], axis=-1, keepdims=True) + jnp.sum(
        row_probs[1] * grad_probs[1], axis=-1, keepdims=True
    )
    grad_scores = [
        (row_probs[n] * (grad_probs[n] - row_inner) * score_scale).astype(jnp.bfloat16)
        for n in range(2)
    ]
    query_grads = jnp.einsum(
        "chij,chjd->chid", grad_scores[0], keys_used[0], preferred_element_type=jnp.float32
    )
    query_grads = query_grads + jnp.einsum(
        "chij,chjd->chid", grad_scores[1], keys_used[1], preferred_element_type=jnp.float32
    )
    grad_queries = to_tokens(out_of_blocks(query_grads.astype(jnp.bfloat16))[None])
    slot_range = jnp.arange(slots, dtype=jnp.int32)
    slot_key = jnp.zeros((slots, heads_here, NBLEN, DH), jnp.float32)
    slot_value = jnp.zeros((slots, heads_here, NBLEN, DH), jnp.float32)
    for n in range(2):
        picker = (block_use[:, n][:, None] == slot_range[None, :]).astype(jnp.bfloat16)
        key_part = jnp.einsum(
            "chij,chid->chjd", grad_scores[n], queries_moved, preferred_element_type=jnp.float32
        ).astype(jnp.bfloat16)
        value_part = jnp.einsum(
            "chij,chid->chjd", probs_low[n], grads_moved, preferred_element_type=jnp.float32
        ).astype(jnp.bfloat16)
        slot_key = slot_key + jnp.einsum(
            "cs,chjd->shjd", picker, key_part, preferred_element_type=jnp.float32
        )
        slot_value = slot_value + jnp.einsum(
            "cs,chjd->shjd", picker, value_part, preferred_element_type=jnp.float32
        )
    slot_grads = jnp.stack([slot_key.astype(jnp.bfloat16), slot_value.astype(jnp.bfloat16)], axis=1)
    slot_grads = slot_grads.transpose(0, 1, 3, 2, 4).reshape(slots, 2, NBLEN, head_width)
    returned = lax.all_to_all(
        slot_grads.reshape(entries.shape + slot_grads.shape[1:]),
        "enc",
        split_axis=0,
        concat_axis=0,
        tiled=True,
    )
    returned = returned.reshape((-1,) + kv_pool.shape[1:])
    owner_pick = (
        entries.reshape(-1)[:, None] == jnp.arange(kv_pool.shape[0], dtype=jnp.int32)[None, :]
    ).astype(jnp.bfloat16)
    pool_grads = jnp.einsum(
        "ep,ekjw->pkjw", owner_pick, returned, preferred_element_type=jnp.float32
    )
    return (context, grad_queries, pool_grads.astype(jnp.bfloat16))


def solution(mesh):
    in_specs = (
        P("enc", "seq", None),
        P("enc", None, None, "seq"),
        P("enc", None, None),
        P("enc", None, None),
        P("enc", "seq", None),
    )
    out_specs = (P("enc", "seq", None), P("enc", "seq", None), P("enc", None, None, "seq"))
    return jax.shard_map(local, mesh=mesh, in_specs=in_specs, out_specs=out_specs, check_vma=False)
```

profile of v0, /device:TPU:1, one launch (start us, length us, event | category | flops | bytes accessed | tf_op | source)
XLA Modules:
  0.0 602.9 jit_solution(16944894643721143449)
XLA Ops:
  0.6 9.6 %copy.57 = bf16[1,128,8192]{1,0,2:T(2,128)(2,1)} copy(bf16[1,128,8192]{2,1,0:T(8,128)(2,1)} %param.5) | data formatting | bytes 4194304 | tf_op args[0]
  10.8 46.5 %reduce = bf16[8192,128]{1,0:T(8,128)(2,1)} reduce(bf16[8192,1,128]{2,1,0:T(2,128)(2,1)} %bitcast.134, bf16[]{:T(256)} %broadcast.101), dimensions={1}, to_apply=%bitcast.102.reduce_sub_computation | reduce | bytes 4194306
  57.3 3.9 reshape.129
  61.2 7.6 %all-to-all-start = ((bf16[16,2,32768]{2,1,0:T(2,128)(2,1)}), bf16[16,2,32768]{2,1,0:T(2,128)(2,1)}, u32[]{:S(2)}, u32[]{:S(2)}) async-start(bf16[16,2,32768]{2,1,0:T(2,128)(2,1)} %reshape.129), calls=%async_computation | async-start | bytes 4194304 | tf_op jit(solution)/shard_map/all_to_all | solution.py:12
  68.9 9.5 %copy.66 = bf16[1,128,8192]{1,0,2:T(2,128)(2,1)} copy(bf16[1,128,8192]{2,1,0:T(8,128)(2,1)} %param.9) | data formatting | bytes 4194304 | tf_op args[4]
  78.3 46.5 %reduce.2 = bf16[8192,128]{1,0:T(8,128)(2,1)} reduce(bf16[8192,1,128]{2,1,0:T(2,128)(2,1)} %bitcast.141, bf16[]{:T(256)} %broadcast.101), dimensions={1}, to_apply=%bitcast.106.reduce_sub_computation | reduce | bytes 4194306
  124.8 4.0 reshape.133
  128.8 6.7 %all-to-all-start.3 = ((bf16[16,2,32768]{2,1,0:T(2,128)(2,1)}), bf16[16,2,32768]{2,1,0:T(2,128)(2,1)}, u32[]{:S(2)}, u32[]{:S(2)}) async-start(bf16[16,2,32768]{2,1,0:T(2,128)(2,1)} %reshape.133), calls=%async_computation.3 | async-start | bytes 4194304 | tf_op jit(solution)/shard_map/all_to_all | solution.py:12
  135.5 2.8 gather_fusion
  138.3 26.0 %all-to-all-done.3 = bf16[16,2,32768]{2,1,0:T(2,128)(2,1)} async-done(((bf16[16,2,32768]{2,1,0:T(2,128)(2,1)}), bf16[16,2,32768]{2,1,0:T(2,128)(2,1)}, u32[]{:S(2)}, u32[]{:S(2)}) %all-to-all-start.3) | async-done | bytes 2097184 | tf_op jit(solution)/shard_map/all_to_all | solution.py:12
  164.2 11.7 %all-to-all-start.1 = ((bf16[16,1,2,128,512]{4,3,2,1,0:T(8,128)(2,1)}), bf16[16,1,2,128,512]{4,3,2,1,0:T(8,128)(2,1)}, u32[]{:S(2)}, u32[]{:S(2)}) async-start(bf16[16,1,2,128,512]{4,3,2,1,0:T(8,128)(2,1)} %bitcast.142), calls=%async_computation.1 | async-start | bytes 8388608 | tf_op jit(solution)/shard_map/all_to_all | solution.py:21
  175.9 10.5 %reshape.130 = bf16[8192,1,128]{2,1,0:T(2,128)(2,1)} reshape(bf16[16,2,32768]{2,1,0:T(2,128)(2,1)} %all-to-all-done) | data formatting | bytes 4194304
  186.4 2.5 copy.85
  188.8 2.6 copy.58
  195.0 2.5 reshape.81
  197.5 10.5 %reshape.134 = bf16[8192,1,128]{2,1,0:T(2,128)(2,1)} reshape(bf16[16,2,32768]{2,1,0:T(2,128)(2,1)} %all-to-all-done.3) | data formatting | bytes 4194304
  208.0 3.8 copy.87
  211.8 3.9 copy.67
  219.2 4.0 reshape.83
  223.1 46.4 %all-to-all-done.1 = bf16[16,1,2,128,512]{4,3,2,1,0:T(8,128)(2,1)} async-done(((bf16[16,1,2,128,512]{4,3,2,1,0:T(8,128)(2,1)}), bf16[16,1,2,128,512]{4,3,2,1,0:T(8,128)(2,1)}, u32[]{:S(2)}, u32[]{:S(2)}) %all-to-all-start.1) | async-done | bytes 4194336 | tf_op jit(solution)/shard_map/all_to_all | solution.py:21
  269.5 6.4 %copy.61 = bf16[16,1,2,128,512]{3,4,2,0,1:T(8,128)(2,1)} copy(bf16[16,1,2,128,512]{4,3,2,1,0:T(8,128)(2,1)} %all-to-all-done.1) | data formatting | bytes 8388608 | tf_op jit(solution)/shard_map/all_to_all | solution.py:21
  275.9 6.2 %copy.62 = bf16[16,2,128,4,128]{4,2,3,0,1:T(8,128)(2,1)} copy(bf16[16,2,128,4,128]{2,4,3,1,0:T(8,128)(2,1)} %bitcast.144) | data formatting | bytes 8388608 | tf_op jit(solution)/shard_map/reshape;reshape | solution.py:49
  282.1 4.8 slice_bitcast_fusion.1
  286.9 4.6 gather_fusion.3
  291.5 4.6 gather_fusion.1
  296.1 4.6 gather_fusion.2
  300.8 4.6 gather_fusion.4
  305.4 5.4 multiply_reduce_fusion.3
  310.9 3.1 multiply_reduce_fusion.2
  314.0 3.8 fusion.14
  317.9 3.9 fusion.53
  321.8 3.0 fusion.40
  327.9 18.5 %copy.158 = bf16[1,2048,512]{2,0,1:T(2,128)(2,1)} copy(bf16[1,2048,512]{2,1,0:T(8,128)(2,1)S(1)} %pad_bitcast_fusion.1) | data formatting | bytes 4194304 | tf_op jit(solution)/shard_map/broadcast_in_dim | solution.py:86
  346.4 15.4 %reduce.1 = bf16[2048,512]{1,0:T(8,128)(2,1)} reduce(bf16[2048,1,512]{2,1,0:T(2,128)(2,1)} %bitcast.138, bf16[]{:T(256)} %broadcast.101), dimensions={1}, to_apply=%bitcast.133.reduce_sub_computation | reduce | bytes 4194306
  361.8 4.5 reshape.131
  366.2 4.7 all-to-all-start.2
  370.9 5.9 fusion.23
  376.9 8.0 %multiply_reduce_fusion = (f32[32,4,64]{2,1,0:T(4,128)S(1)}, f32[32,4,64]{2,1,0:T(4,128)S(1)}, f32[32,4,64,128]{3,2,1,0:T(8,128)}) fusion(f32[32,4,64]{2,1,0:T(4,128)S(1)} %add.65, f32[32,4,64]{2,1,0:T(4,128)S(1)} %max.8, f32[32,4,64,128]{3,2,1,0:T(8,128)S(1)} %copy-done.5, f32[32,4,64,128]{3,2,1,0:T(8,128)S(1)} %fusion.23, ...), kind=kOutput, calls=%fused_computation.22 | convolution fusion | flops 278904832 | bytes 23199744 | tf_op jit(solution)/shard_map/chid,chjd->chij/dot_general | solution.py:90
  385.0 5.4 multiply_convert_fusion
  391.6 3.3 convolution_convert_fusion.2
  399.1 18.9 %copy.157 = bf16[1,2048,512]{2,0,1:T(2,128)(2,1)} copy(bf16[1,2048,512]{2,1,0:T(8,128)(2,1)S(1)} %pad_bitcast_fusion) | data formatting | bytes 4194304 | tf_op jit(solution)/shard_map/broadcast_in_dim | solution.py:106
  418.1 15.4 %reduce.3 = bf16[2048,512]{1,0:T(8,128)(2,1)} reduce(bf16[2048,1,512]{2,1,0:T(2,128)(2,1)} %bitcast.135, bf16[]{:T(256)} %broadcast.101), dimensions={1}, to_apply=%bitcast.132.reduce_sub_computation | reduce | bytes 4194306
  433.4 4.5 reshape.135
  437.9 5.0 convolution_convert_fusion.3
  443.0 5.6 convolution_convert_fusion
  448.5 4.4 fusion.3
  453.0 4.4 fusion.7
  457.3 7.1 %all-to-all-start.4 = ((bf16[16,2,32768]{2,1,0:T(2,128)(2,1)}), bf16[16,2,32768]{2,1,0:T(2,128)(2,1)}, u32[]{:S(2)}, u32[]{:S(2)}) async-start(bf16[16,2,32768]{2,1,0:T(2,128)(2,1)} %reshape.135), calls=%async_computation.4 | async-start | bytes 4194304 | tf_op jit(solution)/shard_map/all_to_all | solution.py:16
  464.4 6.8 %convolution_convert_fusion.1 = bf16[32,4,128,128]{3,2,1,0:T(8,128)(2,1)S(1)} fusion(bf16[32,64,4,128]{3,2,1,0:T(4,128)(2,1)S(1)} %copy-done.18, f32[32,4,64,128]{3,2,1,0:T(8,128)} %copy-done.2, f32[32,4,64]{2,1,0:T(4,128)S(1)} %add.65, f32[32,4,64]{2,1,0:T(4,128)S(1)} %max.8), kind=kOutput, calls=%fused_computation.34 | convolution fusion | flops 274726912 | bytes 10551296 | tf_op jit(solution)/shard_map/chij,chid->chjd/dot_general | solution.py:115
  471.3 2.6 fusion.37
  474.7 2.6 fusion.34
  479.6 7.5 %copy.76 = bf16[16,2,128,4,128]{2,4,3,1,0:T(8,128)(2,1)} copy(bf16[16,2,128,4,128]{4,0,2,3,1:T(8,128)(2,1)} %maximum_bitcast_fusion) | data formatting | bytes 8388608 | tf_op jit(solution)/shard_map/transpose | solution.py:125
  487.1 6.4 %copy.77 = bf16[16,1,2,128,512]{4,3,2,1,0:T(8,128)(2,1)} copy(bf16[16,1,2,128,512]{3,4,2,0,1:T(8,128)(2,1)} %bitcast.145) | data formatting | bytes 8388608 | tf_op jit(solution)/shard_map/reshape;reshape | solution.py:127
  493.5 8.9 %all-to-all-start.5 = ((bf16[16,1,2,128,512]{4,3,2,1,0:T(8,128)(2,1)}), bf16[16,1,2,128,512]{4,3,2,1,0:T(8,128)(2,1)}, u32[]{:S(2)}, u32[]{:S(2)}) async-start(bf16[16,1,2,128,512]{4,3,2,1,0:T(8,128)(2,1)} %copy.77), calls=%async_computation.5 | async-start | bytes 8388608 | tf_op jit(solution)/shard_map/all_to_all | solution.py:126
  502.4 10.5 %reshape.132 = bf16[2048,1,512]{2,1,0:T(2,128)(2,1)} reshape(bf16[16,2,32768]{2,1,0:T(2,128)(2,1)} %all-to-all-done.2) | data formatting | bytes 4194304
  512.9 2.8 copy.86
  515.7 2.4 copy.65
  518.1 4.1 copy.79
  522.1 10.5 %reshape.136 = bf16[2048,1,512]{2,1,0:T(2,128)(2,1)} reshape(bf16[16,2,32768]{2,1,0:T(2,128)(2,1)} %all-to-all-done.4) | data formatting | bytes 4194304
  532.6 2.8 copy.88
  535.4 2.4 copy.71
  537.8 4.1 copy.80
  541.8 54.0 %all-to-all-done.5 = bf16[16,1,2,128,512]{4,3,2,1,0:T(8,128)(2,1)} async-done(((bf16[16,1,2,128,512]{4,3,2,1,0:T(8,128)(2,1)}), bf16[16,1,2,128,512]{4,3,2,1,0:T(8,128)(2,1)}, u32[]{:S(2)}, u32[]{:S(2)}) %all-to-all-start.5) | async-done | bytes 4194336 | tf_op jit(solution)/shard_map/all_to_all | solution.py:126
  595.9 4.7 fusion.31
  (73 shorter events, 21.3 us)
Async XLA Ops:
  0.6 134.8 %copy-start = (bf16[8,2,128,512]{3,2,1,0:T(8,128)(2,1)S(1)}, bf16[8,2,128,512]{3,2,1,0:T(8,128)(2,1)}, u32[]{:S(2)}) copy-start(bf16[8,2,128,512]{3,2,1,0:T(8,128)(2,1)} %param.6) | copy-start | bytes 6291460
  61.2 67.5 %all-to-all-start = ((bf16[16,2,32768]{2,1,0:T(2,128)(2,1)}), bf16[16,2,32768]{2,1,0:T(2,128)(2,1)}, u32[]{:S(2)}, u32[]{:S(2)}) async-start(bf16[16,2,32768]{2,1,0:T(2,128)(2,1)} %reshape.129), calls=%async_computation | async-start | bytes 4194304 | tf_op jit(solution)/shard_map/all_to_all | solution.py:12
  124.8 10.6 %copy-start.21 = (s32[1,16,1]{1,2,0:T(1,128)S(1)}, s32[1,16,1]{1,2,0:T(1,128)}, u32[]{:S(2)}) copy-start(s32[1,16,1]{1,2,0:T(1,128)} %param.7) | copy-start | bytes 196
  128.8 35.5 %all-to-all-start.3 = ((bf16[16,2,32768]{2,1,0:T(2,128)(2,1)}), bf16[16,2,32768]{2,1,0:T(2,128)(2,1)}, u32[]{:S(2)}, u32[]{:S(2)}) async-start(bf16[16,2,32768]{2,1,0:T(2,128)(2,1)} %reshape.133), calls=%async_computation.3 | async-start | bytes 4194304 | tf_op jit(solution)/shard_map/all_to_all | solution.py:12
  164.2 11.7 %copy-start.20 = (s32[1,32,2]{1,2,0:T(2,128)S(1)}, s32[1,32,2]{1,2,0:T(2,128)}, u32[]{:S(2)}) copy-start(s32[1,32,2]{1,2,0:T(2,128)} %param.8) | copy-start | bytes 772
  164.2 105.3 %all-to-all-start.1 = ((bf16[16,1,2,128,512]{4,3,2,1,0:T(8,128)(2,1)}), bf16[16,1,2,128,512]{4,3,2,1,0:T(8,128)(2,1)}, u32[]{:S(2)}, u32[]{:S(2)}) async-start(bf16[16,1,2,128,512]{4,3,2,1,0:T(8,128)(2,1)} %bitcast.142), calls=%async_computation.1 | async-start | bytes 8388608 | tf_op jit(solution)/shard_map/all_to_all | solution.py:21
  305.4 5.4 copy-start.7
  310.8 7.0 %copy-start.2 = (f32[32,4,64,128]{3,2,1,0:T(8,128)}, f32[32,4,64,128]{3,2,1,0:T(8,128)S(1)}, u32[]{:S(2)}) copy-start(f32[32,4,64,128]{3,2,1,0:T(8,128)S(1)} %get-tuple-element.31) | copy-start | bytes 12582916
  314.0 7.8 %copy-start.4 = (f32[32,4,64,128]{3,2,1,0:T(8,128)}, f32[32,4,64,128]{3,2,1,0:T(8,128)S(1)}, u32[]{:S(2)}) copy-start(f32[32,4,64,128]{3,2,1,0:T(8,128)S(1)} %get-tuple-element.33) | copy-start | bytes 12582916
  314.0 3.9 copy-start.11
  317.9 4.0 copy-start.19
  366.2 91.1 %all-to-all-start.2 = ((bf16[16,2,32768]{2,1,0:T(2,128)(2,1)}), bf16[16,2,32768]{2,1,0:T(2,128)(2,1)}, u32[]{:S(2)}, u32[]{:S(2)}) async-start(bf16[16,2,32768]{2,1,0:T(2,128)(2,1)} %reshape.131), calls=%async_computation.2 | async-start | bytes 4194304 | tf_op jit(solution)/shard_map/all_to_all | solution.py:16
  370.9 6.0 copy-start.3
  370.9 6.0 copy-start.5
  370.9 6.0 copy-start.16
  385.0 5.4 copy-start.9
  390.3 1.3 copy-start.10
  391.6 3.3 copy-start.8
  437.9 5.0 copy-start.6
  437.9 5.0 copy-start.17
  448.5 4.4 copy-start.13
  457.3 7.1 %copy-start.18 = (bf16[32,64,4,128]{3,2,1,0:T(4,128)(2,1)S(1)}, bf16[32,64,4,128]{3,2,1,0:T(4,128)(2,1)}, u32[]{:S(2)}) copy-start(bf16[32,64,4,128]{3,2,1,0:T(4,128)(2,1)} %reshape.83) | copy-start | bytes 6291460
  457.3 36.2 %all-to-all-start.4 = ((bf16[16,2,32768]{2,1,0:T(2,128)(2,1)}), bf16[16,2,32768]{2,1,0:T(2,128)(2,1)}, u32[]{:S(2)}, u32[]{:S(2)}) async-start(bf16[16,2,32768]{2,1,0:T(2,128)(2,1)} %reshape.135), calls=%async_computation.4 | async-start | bytes 4194304 | tf_op jit(solution)/shard_map/all_to_all | solution.py:16
  464.4 6.8 %copy-start.15 = (f32[16,4,128,128]{3,0,2,1:T(8,128)S(1)}, f32[16,4,128,128]{3,0,2,1:T(8,128)}, u32[]{:S(2)}) copy-start(f32[16,4,128,128]{3,0,2,1:T(8,128)} %fusion.3) | copy-start | bytes 12582916
  471.2 2.6 copy-start.12
  471.2 3.5 copy-start.14
  493.5 102.3 %all-to-all-start.5 = ((bf16[16,1,2,128,512]{4,3,2,1,0:T(8,128)(2,1)}), bf16[16,1,2,128,512]{4,3,2,1,0:T(8,128)(2,1)}, u32[]{:S(2)}, u32[]{:S(2)}) async-start(bf16[16,1,2,128,512]{4,3,2,1,0:T(8,128)(2,1)} %copy.77), calls=%async_computation.5 | async-start | bytes 8388608 | tf_op jit(solution)/shard_map/all_to_all | solution.py:126
  535.4 60.5 %copy-start.22 = (s32[1,16,1]{1,2,0:T(1,128)S(1)}, s32[1,16,1]{1,2,0:T(1,128)}, u32[]{:S(2)}) copy-start(s32[1,16,1]{1,2,0:T(1,128)} %param.7) | copy-start | bytes 196
  595.9 6.8 %copy-start.1 = (bf16[8,2,128,512]{3,2,1,0:T(8,128)(2,1)S(1)}, bf16[8,2,128,512]{3,2,1,0:T(8,128)(2,1)}, u32[]{:S(2)}) copy-start(bf16[8,2,128,512]{3,2,1,0:T(8,128)(2,1)} %param.6) | copy-start | bytes 6291460
where the time goes:
time: 615 us; the launch traced here: 603 us
  local copies, waits for them, and re-layouts  222 us (36%)
  other arithmetic  135 us (22%)
  waiting for transfers between devices  126 us (20%)
  matrix products  71.4 us (12%)
  starting transfers between devices  46.5 us (8%)
    unnamed x4, other arithmetic  124 us
    unnamed x66, local copies, waits for them, and re-layouts  102 us
    all_to_all x1, waiting for transfers between devices, local(): lax.all_to_all(slot_grads.reshape(entries.shape + slot_grads.shape[1:]),...  54 us
    all_to_all x1, waiting for transfers between devices, fetch_slots(): lax.all_to_all(outgoing, 'enc', split_axis=0, concat_axis=0, tiled=True)  46.4 us
    all_to_all x2, waiting for transfers between devices, to_heads(): lax.all_to_all(token_major, 'seq', split_axis=2, concat_axis=1, tiled=True)  26 us
    broadcast_in_dim x2, local copies, waits for them, and re-layouts, local(): out_of_blocks(query_grads.astype(jnp.bfloat16))[None]  19.4 us
    broadcast_in_dim x2, local copies, waits for them, and re-layouts, local(): context = to_tokens(out_of_blocks(out_blocks.astype(jnp.bfloat16))[None])  19 us
    all_to_all x2, starting transfers between devices, to_heads(): lax.all_to_all(token_major, 'seq', split_axis=2, concat_axis=1, tiled=True)  14.3 us
  transfers between devices with their start and end apart: 6, of which 3 were waited for; matrix products, arithmetic and copies ran while one was open for 44% of the time, Pallas kernels for 0%

commit v1 on v0

--- a/solution.py
+++ b/solution.py
@@ -13,7 +13,10 @@
 
 
 def to_tokens(head_major):
-    return lax.all_to_all(head_major, "seq", split_axis=1, concat_axis=2, tiled=True)
+    return jnp.concatenate(
+        lax.all_to_all(jnp.stack(jnp.split(head_major, lax.axis_size("seq"), axis=1)), "seq", 0, 0),
+        axis=2,
+    )
 
 
 def fetch_slots(kv_pool, entries):

time: 615 us -> 561 us (0.912)
  local copies, waits for them, and re-layouts: 222 us -> 171 us
  other arithmetic: 135 us -> 105 us
  waiting for transfers between devices: 126 us -> 154 us
    unnamed x4 -> x2, other arithmetic: 124 us -> 93 us
    all_to_all x1, waiting for transfers between devices: 54 us -> 81.6 us  [local(): lax.all_to_all(slot_grads.reshape(entries.shape + slot_grads.shape[1:]),...]
    broadcast_in_dim x2 -> x1, local copies, waits for them, and re-layouts: 19.4 us -> 0.49 us  [local(): out_of_blocks(query_grads.astype(jnp.bfloat16))[None]]
    broadcast_in_dim x2 -> x1, local copies, waits for them, and re-layouts: 19 us -> 0.49 us  [local(): context = to_tokens(out_of_blocks(out_blocks.astype(jnp.bfloat16))[None])]
    unnamed x66 -> x82, local copies, waits for them, and re-layouts: 102 us -> 85.9 us
  transfers between devices with their start and end apart: 6 -> 6, of which waited for: 3 -> 3; matrix products, arithmetic and copies ran while one was open for 44% -> 34% of each run, Pallas kernels for 0% -> 0%
where the time goes in v1:
time: 561 us; the launch traced here: 550 us
  local copies, waits for them, and re-layouts  171 us (30%)
  waiting for transfers between devices  154 us (27%)
  other arithmetic  105 us (19%)
  matrix products  71.5 us (13%)
  starting transfers between devices  46.6 us (8%)
    unnamed x2, other arithmetic  93 us
    unnamed x82, local copies, waits for them, and re-layouts  85.9 us
    all_to_all x1, waiting for transfers between devices, local(): lax.all_to_all(slot_grads.reshape(entries.shape + slot_grads.shape[1:]),...  81.6 us
    all_to_all x1, waiting for transfers between devices, fetch_slots(): lax.all_to_all(outgoing, 'enc', split_axis=0, concat_axis=0, tiled=True)  46.4 us
    all_to_all x2, waiting for transfers between devices, to_heads(): lax.all_to_all(token_major, 'seq', split_axis=2, concat_axis=1, tiled=True)  26 us
    all_to_all x2, starting transfers between devices, to_heads(): lax.all_to_all(token_major, 'seq', split_axis=2, concat_axis=1, tiled=True)  14.4 us
    dot_general x2, matrix products, local(): jnp.einsum('chij,chid->chjd', probs_low[n], grads_moved, preferred_elemen...  12.3 us
    all_to_all x1, starting transfers between devices, fetch_slots(): lax.all_to_all(outgoing, 'enc', split_axis=0, concat_axis=0, tiled=True)  11.7 us
  transfers between devices with their start and end apart: 6, of which 3 were waited for; matrix products, arithmetic and copies ran while one was open for 34% of the time, Pallas kernels for 0%

profile of v1, /device:TPU:1, one launch (start us, length us, event | category | flops | bytes accessed | tf_op | source)
XLA Modules:
  0.0 550.1 jit_solution(11700869312573791062)
XLA Ops:
  0.6 9.6 %copy.87 = bf16[1,128,8192]{1,0,2:T(2,128)(2,1)} copy(bf16[1,128,8192]{2,1,0:T(8,128)(2,1)} %param.5) | data formatting | bytes 4194304 | tf_op args[0]
  10.8 46.5 %reduce = bf16[8192,128]{1,0:T(8,128)(2,1)} reduce(bf16[8192,1,128]{2,1,0:T(2,128)(2,1)} %bitcast.250, bf16[]{:T(256)} %broadcast.101), dimensions={1}, to_apply=%bitcast.226.reduce_sub_computation | reduce | bytes 4194306
  57.3 3.9 reshape.145
  61.2 7.6 %all-to-all-start = ((bf16[16,2,32768]{2,1,0:T(2,128)(2,1)}), bf16[16,2,32768]{2,1,0:T(2,128)(2,1)}, u32[]{:S(2)}, u32[]{:S(2)}) async-start(bf16[16,2,32768]{2,1,0:T(2,128)(2,1)} %reshape.145), calls=%async_computation | async-start | bytes 4194304 | tf_op jit(solution)/shard_map/all_to_all | solution.py:12
  68.9 9.5 %copy.95 = bf16[1,128,8192]{1,0,2:T(2,128)(2,1)} copy(bf16[1,128,8192]{2,1,0:T(8,128)(2,1)} %param.9) | data formatting | bytes 4194304 | tf_op args[4]
  78.3 46.5 %reduce.1 = bf16[8192,128]{1,0:T(8,128)(2,1)} reduce(bf16[8192,1,128]{2,1,0:T(2,128)(2,1)} %bitcast.251, bf16[]{:T(256)} %broadcast.101), dimensions={1}, to_apply=%bitcast.228.reduce_sub_computation | reduce | bytes 4194306
  124.8 3.9 reshape.147
  128.8 6.8 %all-to-all-start.3 = ((bf16[16,2,32768]{2,1,0:T(2,128)(2,1)}), bf16[16,2,32768]{2,1,0:T(2,128)(2,1)}, u32[]{:S(2)}, u32[]{:S(2)}) async-start(bf16[16,2,32768]{2,1,0:T(2,128)(2,1)} %reshape.147), calls=%async_computation.3 | async-start | bytes 4194304 | tf_op jit(solution)/shard_map/all_to_all | solution.py:12
  135.6 2.8 gather_fusion
  138.4 26.0 %all-to-all-done.3 = bf16[16,2,32768]{2,1,0:T(2,128)(2,1)} async-done(((bf16[16,2,32768]{2,1,0:T(2,128)(2,1)}), bf16[16,2,32768]{2,1,0:T(2,128)(2,1)}, u32[]{:S(2)}, u32[]{:S(2)}) %all-to-all-start.3) | async-done | bytes 2097184 | tf_op jit(solution)/shard_map/all_to_all | solution.py:12
  164.4 11.7 %all-to-all-start.1 = ((bf16[16,1,2,128,512]{4,3,2,1,0:T(8,128)(2,1)}), bf16[16,1,2,128,512]{4,3,2,1,0:T(8,128)(2,1)}, u32[]{:S(2)}, u32[]{:S(2)}) async-start(bf16[16,1,2,128,512]{4,3,2,1,0:T(8,128)(2,1)} %bitcast.254), calls=%async_computation.1 | async-start | bytes 8388608 | tf_op jit(solution)/shard_map/all_to_all | solution.py:24
  176.1 10.4 %reshape.146 = bf16[8192,1,128]{2,1,0:T(2,128)(2,1)} reshape(bf16[16,2,32768]{2,1,0:T(2,128)(2,1)} %all-to-all-done) | data formatting | bytes 4194304
  186.5 2.5 copy.113
  189.0 2.6 copy.88
  191.6 2.1 slice.48
  193.7 1.5 concatenate.12
  195.1 2.5 reshape.93
  197.7 10.4 %reshape.148 = bf16[8192,1,128]{2,1,0:T(2,128)(2,1)} reshape(bf16[16,2,32768]{2,1,0:T(2,128)(2,1)} %all-to-all-done.3) | data formatting | bytes 4194304
  208.1 3.8 copy.114
  211.9 3.9 copy.96
  215.8 2.1 slice.52
  219.3 4.0 reshape.97
  223.3 46.4 %all-to-all-done.1 = bf16[16,1,2,128,512]{4,3,2,1,0:T(8,128)(2,1)} async-done(((bf16[16,1,2,128,512]{4,3,2,1,0:T(8,128)(2,1)}), bf16[16,1,2,128,512]{4,3,2,1,0:T(8,128)(2,1)}, u32[]{:S(2)}, u32[]{:S(2)}) %all-to-all-start.1) | async-done | bytes 4194336 | tf_op jit(solution)/shard_map/all_to_all | solution.py:24
  269.7 6.4 %copy.91 = bf16[16,1,2,128,512]{3,4,2,0,1:T(8,128)(2,1)} copy(bf16[16,1,2,128,512]{4,3,2,1,0:T(8,128)(2,1)} %all-to-all-done.1) | data formatting | bytes 8388608 | tf_op jit(solution)/shard_map/all_to_all | solution.py:24
  276.1 6.2 %copy.92 = bf16[16,2,128,4,128]{4,2,3,0,1:T(8,128)(2,1)} copy(bf16[16,2,128,4,128]{2,4,3,1,0:T(8,128)(2,1)} %bitcast.256) | data formatting | bytes 8388608 | tf_op jit(solution)/shard_map/reshape;reshape | solution.py:52
  282.3 4.8 slice_bitcast_fusion.1
  287.1 4.6 gather_fusion.3
  291.7 4.6 gather_fusion.1
  296.3 4.6 gather_fusion.2
  301.0 4.6 gather_fusion.4
  305.6 5.4 multiply_reduce_fusion.3
  311.0 3.1 multiply_reduce_fusion.2
  314.2 3.8 fusion.14
  318.1 4.7 fusion.53
  322.7 3.0 fusion.23
  325.7 8.0 %multiply_reduce_fusion = (f32[32,4,64]{2,1,0:T(4,128)S(1)}, f32[32,4,64]{2,1,0:T(4,128)S(1)}, f32[32,4,64,128]{3,2,1,0:T(8,128)}) fusion(f32[32,4,64]{2,1,0:T(4,128)S(1)} %add.65, f32[32,4,64]{2,1,0:T(4,128)S(1)} %max.8, f32[32,4,64,128]{3,2,1,0:T(8,128)S(1)} %get-tuple-element.33, f32[32,4,64,128]{3,2,1,0:T(8,128)S(1)} %fusion.23, ...), kind=kOutput, calls=%fused_computation.22 | convolution fusion | flops 278904832 | bytes 23199744 | tf_op jit(solution)/shard_map/chid,chjd->chij/dot_general | solution.py:93
  333.8 6.2 %multiply_convert_fusion = (bf16[32,4,64,128]{3,2,1,0:T(8,128)(2,1)}, bf16[32,4,64,128]{3,2,1,0:T(8,128)(2,1)S(1)}) fusion(f32[32,4,64,128]{3,2,1,0:T(8,128)} %get-tuple-element.34, f32[32,4,64]{2,1,0:T(4,128)S(1)} %add.67, f32[32,4,64]{2,1,0:T(4,128)S(1)} %add.65, f32[32,4,64]{2,1,0:T(4,128)S(1)} %max.8, f32[32,4,64,128]{3,2,1,0:T(8,128)S(1)} %get-tuple-element.33, ...), kind=kLoop, calls=%fused_computation.20 | loop fusion | flops 14680064 | bytes 21069824 | tf_op jit(solution)/shard_map/convert_element_type | solution.py:100
  340.0 3.2 fusion.107
  343.2 3.5 convolution_convert_fusion.3
  346.7 1.5 copy-done.18
  348.2 3.0 fusion.40
  351.2 2.0 copy.93
  364.8 4.6 all-to-all-start.2
  369.5 3.1 convolution_convert_fusion.2
  372.9 3.5 fusion.41
  376.4 2.0 copy.98
  390.1 5.5 convolution_convert_fusion
  395.6 4.4 fusion.3
  400.0 4.4 fusion.7
  404.4 7.0 %all-to-all-start.4 = ((bf16[16,1,128,512]{3,2,1,0:T(8,128)(2,1)}), bf16[16,1,128,512]{3,2,1,0:T(8,128)(2,1)}, u32[]{:S(2)}, u32[]{:S(2)}) async-start(bf16[16,1,128,512]{3,2,1,0:T(8,128)(2,1)} %fusion.55), calls=%async_computation.4 | async-start | bytes 4194304 | tf_op jit(solution)/shard_map/all_to_all | solution.py:17
  411.4 6.8 %convolution_convert_fusion.1 = bf16[32,4,128,128]{3,2,1,0:T(8,128)(2,1)S(1)} fusion(bf16[32,64,4,128]{3,2,1,0:T(4,128)(2,1)S(1)} %copy-done.14, f32[32,4,64,128]{3,2,1,0:T(8,128)} %copy-done.2, f32[32,4,64]{2,1,0:T(4,128)S(1)} %add.65, f32[32,4,64]{2,1,0:T(4,128)S(1)} %max.8), kind=kOutput, calls=%fused_computation.34 | convolution fusion | flops 274726912 | bytes 10551296 | tf_op jit(solution)/shard_map/chij,chid->chjd/dot_general | solution.py:118
  418.2 2.6 fusion.37
  421.6 2.6 fusion.34
  424.3 2.3 maximum_bitcast_fusion
  426.6 7.5 %copy.104 = bf16[16,2,128,4,128]{2,4,3,1,0:T(8,128)(2,1)} copy(bf16[16,2,128,4,128]{4,0,2,3,1:T(8,128)(2,1)} %maximum_bitcast_fusion) | data formatting | bytes 8388608 | tf_op jit(solution)/shard_map/transpose | solution.py:128
  434.1 6.4 %copy.105 = bf16[16,1,2,128,512]{4,3,2,1,0:T(8,128)(2,1)} copy(bf16[16,1,2,128,512]{3,4,2,0,1:T(8,128)(2,1)} %bitcast.257) | data formatting | bytes 8388608 | tf_op jit(solution)/shard_map/reshape;reshape | solution.py:130
  440.5 8.9 %all-to-all-start.5 = ((bf16[16,1,2,128,512]{4,3,2,1,0:T(8,128)(2,1)}), bf16[16,1,2,128,512]{4,3,2,1,0:T(8,128)(2,1)}, u32[]{:S(2)}, u32[]{:S(2)}) async-start(bf16[16,1,2,128,512]{4,3,2,1,0:T(8,128)(2,1)} %copy.105), calls=%async_computation.5 | async-start | bytes 8388608 | tf_op jit(solution)/shard_map/all_to_all | solution.py:129
  449.4 3.0 copy.94
  452.5 2.9 copy.107
  455.4 3.0 copy.99
  458.4 2.9 copy.108
  461.3 81.6 %all-to-all-done.5 = bf16[16,1,2,128,512]{4,3,2,1,0:T(8,128)(2,1)} async-done(((bf16[16,1,2,128,512]{4,3,2,1,0:T(8,128)(2,1)}), bf16[16,1,2,128,512]{4,3,2,1,0:T(8,128)(2,1)}, u32[]{:S(2)}, u32[]{:S(2)}) %all-to-all-start.5) | async-done | bytes 4194336 | tf_op jit(solution)/shard_map/all_to_all | solution.py:129
  542.8 4.7 fusion.31
  547.6 2.0 copy.109
  (87 shorter events, 26.6 us)
Async XLA Ops:
  0.6 135.0 %copy-start = (bf16[8,2,128,512]{3,2,1,0:T(8,128)(2,1)S(1)}, bf16[8,2,128,512]{3,2,1,0:T(8,128)(2,1)}, u32[]{:S(2)}) copy-start(bf16[8,2,128,512]{3,2,1,0:T(8,128)(2,1)} %param.6) | copy-start | bytes 6291460
  61.2 67.6 %all-to-all-start = ((bf16[16,2,32768]{2,1,0:T(2,128)(2,1)}), bf16[16,2,32768]{2,1,0:T(2,128)(2,1)}, u32[]{:S(2)}, u32[]{:S(2)}) async-start(bf16[16,2,32768]{2,1,0:T(2,128)(2,1)} %reshape.145), calls=%async_computation | async-start | bytes 4194304 | tf_op jit(solution)/shard_map/all_to_all | solution.py:12
  128.8 6.8 %copy-start.17 = (s32[1,16,1]{1,2,0:T(1,128)S(1)}, s32[1,16,1]{1,2,0:T(1,128)}, u32[]{:S(2)}) copy-start(s32[1,16,1]{1,2,0:T(1,128)} %param.7) | copy-start | bytes 196
  128.8 35.6 %all-to-all-start.3 = ((bf16[16,2,32768]{2,1,0:T(2,128)(2,1)}), bf16[16,2,32768]{2,1,0:T(2,128)(2,1)}, u32[]{:S(2)}, u32[]{:S(2)}) async-start(bf16[16,2,32768]{2,1,0:T(2,128)(2,1)} %reshape.147), calls=%async_computation.3 | async-start | bytes 4194304 | tf_op jit(solution)/shard_map/all_to_all | solution.py:12
  164.4 11.7 %copy-start.16 = (s32[1,32,2]{1,2,0:T(2,128)S(1)}, s32[1,32,2]{1,2,0:T(2,128)}, u32[]{:S(2)}) copy-start(s32[1,32,2]{1,2,0:T(2,128)} %param.8) | copy-start | bytes 772
  164.4 105.3 %all-to-all-start.1 = ((bf16[16,1,2,128,512]{4,3,2,1,0:T(8,128)(2,1)}), bf16[16,1,2,128,512]{4,3,2,1,0:T(8,128)(2,1)}, u32[]{:S(2)}, u32[]{:S(2)}) async-start(bf16[16,1,2,128,512]{4,3,2,1,0:T(8,128)(2,1)} %bitcast.254), calls=%async_computation.1 | async-start | bytes 8388608 | tf_op jit(solution)/shard_map/all_to_all | solution.py:24
  305.6 5.4 copy-start.5
  311.0 22.7 %copy-start.2 = (f32[32,4,64,128]{3,2,1,0:T(8,128)}, f32[32,4,64,128]{3,2,1,0:T(8,128)S(1)}, u32[]{:S(2)}) copy-start(f32[32,4,64,128]{3,2,1,0:T(8,128)S(1)} %get-tuple-element.31) | copy-start | bytes 12582916
  314.2 32.6 %copy-start.3 = (f32[32,4,64,128]{3,2,1,0:T(8,128)}, f32[32,4,64,128]{3,2,1,0:T(8,128)S(1)}, u32[]{:S(2)}) copy-start(f32[32,4,64,128]{3,2,1,0:T(8,128)S(1)} %get-tuple-element.33) | copy-start | bytes 12582916
  314.2 3.9 copy-start.10
  318.1 4.7 copy-start.13
  333.8 6.3 %copy-start.7 = (bf16[32,4,128,128]{3,2,1,0:T(8,128)(2,1)S(1)}, bf16[32,4,128,128]{3,2,1,0:T(8,128)(2,1)}, u32[]{:S(2)}) copy-start(bf16[32,4,128,128]{3,2,1,0:T(8,128)(2,1)} %gather_fusion.1) | copy-start | bytes 12582916
  343.2 3.5 copy-start.15
  343.2 5.0 copy-start.18
  364.8 39.6 %all-to-all-start.2 = ((bf16[16,1,128,512]{3,2,1,0:T(8,128)(2,1)}), bf16[16,1,128,512]{3,2,1,0:T(8,128)(2,1)}, u32[]{:S(2)}, u32[]{:S(2)}) async-start(bf16[16,1,128,512]{3,2,1,0:T(8,128)(2,1)} %fusion.71), calls=%async_computation.2 | async-start | bytes 4194304 | tf_op jit(solution)/shard_map/all_to_all | solution.py:17
  369.4 3.1 copy-start.6
  369.4 3.5 copy-start.8
  378.9 11.1 %copy-start.4 = (f32[32,4,64,128]{3,2,1,0:T(8,128)S(1)}, f32[32,4,64,128]{3,2,1,0:T(8,128)}, u32[]{:S(2)}) copy-start(f32[32,4,64,128]{3,2,1,0:T(8,128)} %copy-done.3) | copy-start | bytes 12582916
  379.4 10.6 %copy-start.14 = (bf16[32,64,4,128]{3,2,1,0:T(4,128)(2,1)S(1)}, bf16[32,64,4,128]{3,2,1,0:T(4,128)(2,1)}, u32[]{:S(2)}) copy-start(bf16[32,64,4,128]{3,2,1,0:T(4,128)(2,1)} %reshape.97) | copy-start | bytes 6291460
  404.4 36.1 %all-to-all-start.4 = ((bf16[16,1,128,512]{3,2,1,0:T(8,128)(2,1)}), bf16[16,1,128,512]{3,2,1,0:T(8,128)(2,1)}, u32[]{:S(2)}, u32[]{:S(2)}) async-start(bf16[16,1,128,512]{3,2,1,0:T(8,128)(2,1)} %fusion.55), calls=%async_computation.4 | async-start | bytes 4194304 | tf_op jit(solution)/shard_map/all_to_all | solution.py:17
  411.4 6.8 %copy-start.12 = (f32[16,4,128,128]{3,0,2,1:T(8,128)S(1)}, f32[16,4,128,128]{3,0,2,1:T(8,128)}, u32[]{:S(2)}) copy-start(f32[16,4,128,128]{3,0,2,1:T(8,128)} %fusion.3) | copy-start | bytes 12582916
  418.2 2.6 copy-start.9
  418.2 3.5 copy-start.11
  440.5 102.4 %all-to-all-start.5 = ((bf16[16,1,2,128,512]{4,3,2,1,0:T(8,128)(2,1)}), bf16[16,1,2,128,512]{4,3,2,1,0:T(8,128)(2,1)}, u32[]{:S(2)}, u32[]{:S(2)}) async-start(bf16[16,1,2,128,512]{4,3,2,1,0:T(8,128)(2,1)} %copy.105), calls=%async_computation.5 | async-start | bytes 8388608 | tf_op jit(solution)/shard_map/all_to_all | solution.py:129
  542.8 6.8 %copy-start.1 = (bf16[8,2,128,512]{3,2,1,0:T(8,128)(2,1)S(1)}, bf16[8,2,128,512]{3,2,1,0:T(8,128)(2,1)}, u32[]{:S(2)}) copy-start(bf16[8,2,128,512]{3,2,1,0:T(8,128)(2,1)} %param.6) | copy-start | bytes 6291460
